TPU v7x, 32 devices: a whole 2x2x4 slice. The times are simulated.
32 devices in a mesh: groups: 2 (over y), ctx: 8 (over z, core), chan: 2 (over x).
Axes of the slice: x: 2, y: 2, z: 4, core: 2. Of those that a mesh axis runs over, the one named last changes fastest.
Arguments:
- tokens: bfloat16 [4096, 2048], P(('groups', 'ctx')), parts along dimension 0, may hold values from -6 to 6
- in_weight: bfloat16 [2048, 3, 2048], P('ctx', None, 'chan'), may hold values from -0.125 to 0.125
- short_taps: bfloat16 [3, 3, 2048], P(None, None, 'chan'), may hold values from -3.5 to 3.5
- filters: bfloat16 [2048, 2048], P('chan', 'ctx'), may hold values from -0.125 to 0.125
- doc_lengths: int32 [8], P('groups'), parts along dimension 0, may hold values from 1 to 1024, 2048 in all
- out_weight: bfloat16 [2048, 2048], P('chan', 'ctx'), may hold values from -0.125 to 0.125
Outputs:
- output: bfloat16 [4096, 2048], P(('groups', 'ctx', 'chan')), parts along dimension 0
There are 2 independent parts, one for each index of `groups`. A program takes and returns all parts, laid end to end along the dimension named above; an argument that names none is the same for every part. Nothing has to cross between parts.
Inputs may be any that keep to these rules, and one draw needn't show every extreme that they name: doc_lengths are the lengths of the solutions packed one after another; they fill all 2048 positions.
All inputs are finite; a program needn't handle non-finite values.
Results may differ from a plain program's by a relative error of at most 0.007.
Values may be sent and summed in bfloat16 or wider, within the bound.
A program may use at most 64 MiB of HBM per device.

v0:
```python
import math

import jax
import jax.numpy as jnp
from jax import lax
from jax.sharding import PartitionSpec as P


def contract(form, left, right):
    return jnp.einsum(form, left, right, precision=lax.Precision.HIGHEST)


def angle_table(rows, cols, period):
    product = lax.broadcasted_iota(jnp.int32, (rows, cols), 0) * lax.broadcasted_iota(
        jnp.int32, (rows, cols), 1
    )
    theta = (product % period).astype(jnp.float32) * (2.0 * math.pi / period)
    return (jnp.cos(theta), jnp.sin(theta))


def document_ids(doc_lengths, seq_len):
    ends = jnp.cumsum(doc_lengths, dtype=jnp.int32)
    places = lax.broadcasted_iota(jnp.int32, (seq_len, ends.shape[0]), 0)
    return jnp.sum((places >= ends[None, :]).astype(jnp.int32), axis=1)


def short_conv(streams, taps, doc_id):
    result = taps[:, 0, :, None] * streams
    for lag in (1, 2):
        moved = jnp.pad(streams, ((0, 0), (0, 0), (lag, 0)))[:, :, :-lag]
        linked = jnp.concatenate((jnp.zeros((lag,), bool), doc_id[lag:] == doc_id[:-lag]))
        result = result + taps[:, lag, :, None] * jnp.where(linked[None, None, :], moved, 0.0)
    return result


def causal_filter(gated, kernel_rows):
    count, seq_len = gated.shape
    width = math.gcd(seq_len, 128)
    half = seq_len // width
    span = 2 * half
    total = span * width
    signal = gated.reshape(count, half, width)
    kernel = kernel_rows.reshape(count, half, width)
    cos_b, sin_b = angle_table(span, span, span)
    twist_c, twist_s = angle_table(span, width, total)
    cos_a, sin_a = angle_table(width, width, width)

    def forward(values):
        padded = jnp.concatenate((values, jnp.zeros_like(values)), 1)
        real_part = contract("kb,cba->cka", cos_b, padded)
        imag_part = -contract("kb,cba->cka", sin_b, padded)
        turned_r = real_part * twist_c + imag_part * twist_s
        turned_i = imag_part * twist_c - real_part * twist_s
        spec_r = contract("cka,aj->ckj", turned_r, cos_a) + contract("cka,aj->ckj", turned_i, sin_a)
        spec_i = contract("cka,aj->ckj", turned_i, cos_a) - contract("cka,aj->ckj", turned_r, sin_a)
        return (spec_r, spec_i)

    sig_r, sig_i = forward(signal)
    ker_r, ker_i = forward(kernel)
    prod_r = sig_r * ker_r - sig_i * ker_i
    prod_i = sig_r * ker_i + sig_i * ker_r
    back_r = contract("ckj,aj->cka", prod_r, cos_a) - contract("ckj,aj->cka", prod_i, sin_a)
    back_i = contract("ckj,aj->cka", prod_i, cos_a) + contract("ckj,aj->cka", prod_r, sin_a)
    untwist_r = back_r * twist_c - back_i * twist_s
    untwist_i = back_i * twist_c + back_r * twist_s
    blocks = contract("bk,cka->cba", cos_b, untwist_r) - contract("bk,cka->cba", sin_b, untwist_i)
    blocks = blocks[:, :half]
    return (blocks / total).reshape(count, seq_len)


def shards(tokens, in_weight, short_taps, filters, doc_lengths, out_weight):
    width_dev = in_weight.shape[2]
    group_width = width_dev // lax.axis_size("ctx")
    streams = jnp.einsum(
        "dsc,td->sct",
        lax.all_gather(in_weight, "ctx", axis=0, tiled=True),
        tokens,
        preferred_element_type=jnp.float32,
    )
    packed = jnp.concatenate((streams.astype(jnp.bfloat16), filters[None]), 0)
    spread = lax.all_to_all(packed, "ctx", split_axis=1, concat_axis=2, tiled=True)
    taps = lax.dynamic_slice_in_dim(
        short_taps, lax.axis_index("ctx") * group_width, group_width, 2
    ).astype(jnp.float32)
    seq_len = spread.shape[2]
    doc_id = document_ids(doc_lengths, seq_len)
    conv = short_conv(spread[:3].astype(jnp.float32), taps, doc_id)
    filtered = causal_filter(conv[0] * conv[2], spread[3].astype(jnp.float32))
    mixed = (conv[1] * filtered).astype(jnp.bfloat16)
    returned = lax.all_to_all(mixed, "ctx", split_axis=1, concat_axis=0, tiled=True)
    partial_out = lax.dot_general(
        returned,
        lax.all_gather(out_weight, "ctx", axis=1, tiled=True),
        (((0,), (0,)), ((), ())),
        preferred_element_type=jnp.float32,
    )
    return lax.psum_scatter(partial_out, "chan", scatter_dimension=0, tiled=True).astype(
        jnp.bfloat16
    )


def solution(mesh):
    placed = (
        P(("groups", "ctx"), None),
        P("ctx", None, "chan"),
        P(None, None, "chan"),
        P("chan", "ctx"),
        P("groups"),
        P("chan", "ctx"),
    )
    return jax.shard_map(
        shards,
        mesh=mesh,
        in_specs=placed,
        out_specs=P(("groups", "ctx", "chan"), None),
        check_vma=False,
    )
```

profile of v0, /device:TPU:0, one launch (start us, length us, event | category | flops | bytes accessed | tf_op | source)
XLA Modules:
  0.0 361.4 jit_solution(6241623876197891047)
XLA Ops:
  6.5 2.7 copy.77
  9.3 120.0 %all-gather.3.cloned.1.call-done = bf16[2048,3,1024]{0,2,1:T(8,128)(2,1)} async-done(((bf16[256,3,1024]{0,2,1:T(8,128)(2,1)}), bf16[2048,3,1024]{0,2,1:T(8,128)(2,1)}) %all-gather.3.cloned.1.call-update) | async-done | bytes 12582928 | tf_op jit(solution)/shard_map/all_gather | solution.py:76
  129.3 8.1 %convolution_convert_fusion = bf16[3,1024,256]{2,1,0:T(8,128)(2,1)S(1)} fusion(bf16[2048,3,1024]{0,2,1:T(8,128)(2,1)} %all-gather.3.cloned.1.call-done, bf16[256,2048]{1,0:T(8,128)(2,1)S(1)} %copy-done), kind=kOutput, calls=%fused_computation.60 | convolution fusion | flops 3222011904 | bytes 15204352 | tf_op jit(solution)/shard_map/dsc,td->sct/dot_general | solution.py:74
  137.3 0.2 pad_maximum_fusion
  137.5 3.0 copy.78
  140.5 3.7 %all-to-all-start = ((bf16[4,1024,256]{2,0,1:T(4,128)(2,1)}), bf16[4,1024,256]{2,0,1:T(4,128)(2,1)S(1)}, u32[]{:S(2)}, u32[]{:S(2)}) async-start(bf16[4,1024,256]{2,0,1:T(4,128)(2,1)} %copy.78), calls=%async_computation | async-start | bytes 4194304 | tf_op jit(solution)/shard_map/all_to_all | solution.py:81
  144.3 0.7 all-gather.5.cloned.1.call-update
  145.0 0.7 dynamic-slice_convert_fusion
  145.7 0.2 reduce-window.8
  146.4 79.9 %all-to-all-done = bf16[4,1024,256]{2,0,1:T(4,128)(2,1)S(1)} async-done(((bf16[4,1024,256]{2,0,1:T(4,128)(2,1)}), bf16[4,1024,256]{2,0,1:T(4,128)(2,1)S(1)}, u32[]{:S(2)}, u32[]{:S(2)}) %all-to-all-start) | async-done | bytes 2097184 | tf_op jit(solution)/shard_map/all_to_all | solution.py:81
  226.3 0.3 copy.79
  226.6 2.1 slice_convert_fusion
  228.7 0.8 slice.73
  229.5 2.4 copy.80
  231.9 2.3 fusion.3
  234.2 1.2 slice_multiply_fusion.1
  235.3 0.5 copy.103
  235.8 1.9 fusion.8
  237.7 3.2 fusion.6
  240.9 2.7 copy.95
  243.6 0.3 copy.84
  243.9 0.2 convert_element_type.109
  244.1 1.0 fusion.68
  245.1 0.6 copy-done.2
  245.7 2.1 fusion.10
  247.8 3.5 fusion.30
  251.3 3.9 %fusion.32 = f32[128,32,128]{2,0,1:T(8,128)S(1)} fusion(f32[128,32,128]{2,1,0:T(8,128)S(1)} %get-tuple-element.8), kind=kOutput, calls=%fused_computation.46 | convolution fusion | flops 805535744 | bytes 4194304 | tf_op jit(solution)/shard_map/cka,aj->ckj/dot_general | solution.py:10
  255.3 3.6 fusion.40
  258.9 3.5 fusion.38
  262.4 3.7 %fusion.57 = f32[128,32,128]{2,0,1:T(8,128)S(1)} fusion(f32[128,32,128]{2,0,1:T(8,128)S(1)} %fusion.30, f32[128,32,128]{2,1,0:T(8,128)S(1)} %get-tuple-element.7), kind=kOutput, calls=%fused_computation.64 | convolution fusion | flops 806060032 | bytes 6291456 | tf_op jit(solution)/shard_map/cka,aj->ckj/dot_general | solution.py:10
  266.1 3.5 fusion.54
  269.6 3.6 fusion.48
  273.2 4.0 %multiply_subtract_fusion = (f32[128,32,128]{2,0,1:T(8,128)S(1)}, f32[128,32,128]{2,0,1:T(8,128)S(1)}) fusion(f32[128,32,128]{2,0,1:T(8,128)S(1)} %fusion.57, f32[128,32,128]{2,0,1:T(8,128)S(1)} %fusion.48, f32[128,32,128]{2,0,1:T(8,128)S(1)} %fusion.54, f32[128,32,128]{2,0,1:T(8,128)S(1)} %fusion.38, f32[128,32,128]{2,1,0:T(8,128)S(1)} %get-tuple-element.14), kind=kOutput, calls=%fused_computation.35 | convolution fusion | flops 809205760 | bytes 14680064 | tf_op jit(solution)/shard_map/cka,aj->ckj/dot_general | solution.py:10
  277.3 3.4 fusion.24
  280.6 3.4 fusion.22
  284.0 3.4 fusion.60
  287.4 3.7 %fusion.63 = f32[128,32,128]{2,1,0:T(8,128)S(1)} fusion(f32[128,32,128]{2,1,0:T(8,128)S(1)} %fusion.22, f32[128,32,128]{2,0,1:T(8,128)S(1)} %get-tuple-element.5), kind=kOutput, calls=%fused_computation.66 | convolution fusion | flops 806060032 | bytes 6291456 | tf_op jit(solution)/shard_map/ckj,aj->cka/dot_general | solution.py:10
  291.1 2.2 fusion.14
  293.3 2.2 subtract_bitcast_fusion
  295.6 0.1 slice_multiply_fusion
  295.7 0.3 reshape.78
  296.0 0.8 copy-done.3
  296.8 1.1 fusion.71
  297.9 3.5 all-to-all-start.1
  301.5 15.2 %all-to-all-done.1 = bf16[128,8,256]{2,0,1:T(8,128)(2,1)S(1)} async-done(((bf16[128,8,256]{2,0,1:T(8,128)(2,1)}), bf16[128,8,256]{2,0,1:T(8,128)(2,1)S(1)}, u32[]{:S(2)}, u32[]{:S(2)}) %all-to-all-start.1) | async-done | bytes 524320 | tf_op jit(solution)/shard_map/all_to_all | solution.py:90
  316.7 4.9 %fusion.213 = f32[256,2048]{1,0:T(8,128)} fusion(bf16[1024,256]{1,0:T(8,128)(2,1)S(1)} %bitcast.106, bf16[1024,2048]{1,0:T(8,128)(2,1)} %all-gather.5.cloned.1.call-done), kind=kOutput, calls=%fused_computation.218 | convolution fusion | flops 1073741824 | bytes 6815744 | tf_op jit(solution)/shard_map/dot_general | solution.py:91
  321.6 30.8 %reduce-scatter.2.cloned.1.call-done = f32[128,2048]{1,0:T(8,128)} async-done(((f32[256,2048]{1,0:T(8,128)}), f32[128,2048]{1,0:T(8,128)}) %reduce-scatter.2.cloned.1.call-update) | async-done | bytes 1048592 | tf_op jit(solution)/shard_map/reduce_scatter | solution.py:97
  352.4 2.1 convert_element_type.111
  (27 shorter events, 0.7 us)
Async XLA Ops:
  6.5 122.7 %copy-start = (bf16[256,2048]{1,0:T(8,128)(2,1)S(1)}, bf16[256,2048]{1,0:T(8,128)(2,1)}, u32[]{:S(2)}) copy-start(bf16[256,2048]{1,0:T(8,128)(2,1)} %param.6) | copy-start | bytes 3145732
  6.5 122.7 %all-gather.3.cloned.1.call-start = ((), (), s32[]{:S(2)}) async-start(), calls=%async_computation.3 | async-start | bytes 14155776 | tf_op jit(solution)/shard_map/all_gather | solution.py:76
  9.2 128.1 %copy-start.5 = (bf16[1024,256]{1,0:T(8,128)(2,1)S(1)}, bf16[1024,256]{1,0:T(8,128)(2,1)}, u32[]{:S(2)}) copy-start(bf16[1024,256]{1,0:T(8,128)(2,1)} %param.9) | copy-start | bytes 1572868
  140.5 5.2 %copy-start.6 = (s32[4]{0:T(128)S(1)}, s32[4]{0:T(128)}, u32[]{:S(2)}) copy-start(s32[4]{0:T(128)} %param.10) | copy-start | bytes 52
  140.5 85.8 %all-to-all-start = ((bf16[4,1024,256]{2,0,1:T(4,128)(2,1)}), bf16[4,1024,256]{2,0,1:T(4,128)(2,1)S(1)}, u32[]{:S(2)}, u32[]{:S(2)}) async-start(bf16[4,1024,256]{2,0,1:T(4,128)(2,1)} %copy.78), calls=%async_computation | async-start | bytes 4194304 | tf_op jit(solution)/shard_map/all_to_all | solution.py:81
  144.2 157.2 %all-gather.5.cloned.1.call-start = ((), (), s32[]{:S(2)}) async-start(), calls=%async_computation.4 | async-start | bytes 4718592 | tf_op jit(solution)/shard_map/all_gather | solution.py:93
  240.9 2.7 copy-start.4
  244.1 1.6 copy-start.2
  295.5 1.2 copy-start.3
  297.9 18.8 %all-to-all-start.1 = ((bf16[128,8,256]{2,0,1:T(8,128)(2,1)}), bf16[128,8,256]{2,0,1:T(8,128)(2,1)S(1)}, u32[]{:S(2)}, u32[]{:S(2)}) async-start(bf16[128,8,256]{2,0,1:T(8,128)(2,1)} %fusion.71), calls=%async_computation.1 | async-start | bytes 1048576 | tf_op jit(solution)/shard_map/all_to_all | solution.py:90
  301.4 51.0 %reduce-scatter.2.cloned.1.call-start = ((), (), s32[]{:S(2)}) async-start(), calls=%async_computation.5 | async-start | bytes 3145728 | tf_op jit(solution)/shard_map/reduce_scatter | solution.py:97
  316.7 37.8 %copy-start.1 = (bf16[256,2048]{1,0:T(8,128)(2,1)S(1)}, bf16[256,2048]{1,0:T(8,128)(2,1)}, u32[]{:S(2)}) copy-start(bf16[256,2048]{1,0:T(8,128)(2,1)} %param.6) | copy-start | bytes 3145732
Sparse Core Ops, SparseCore 0:
  9.4 119.8 all-gather.2
  146.7 82.0 all-gather.4
  321.7 30.6 reduce-scatter.1
where the time goes:
time: 368 us; the launch traced here: 361 us
  waiting for transfers between devices  247 us (67%)
  matrix products  68.8 us (19%)
  local copies, waits for them, and re-layouts  14.5 us (4%)
  between operations  13.8 us (4%)
  other arithmetic  10.3 us (3%)
  starting transfers between devices  7.31 us (2%)
    all_gather x1, waiting for transfers between devices, shards(): lax.all_gather(in_weight, 'ctx', axis=0, tiled=True)  120 us
    all_to_all x1, waiting for transfers between devices, shards(): lax.all_to_all(packed, 'ctx', split_axis=1, concat_axis=2, tiled=True)  79.9 us
    dot_general x18, matrix products, contract(): return jnp.einsum(form, left, right, precision=lax.Precision.HIGHEST)  55.9 us
    reduce_scatter x1, waiting for transfers between devices, shards(): lax.psum_scatter(partial_out, 'chan', scatter_dimension=0, tiled=True)  30.8 us
    all_to_all x1, waiting for transfers between devices, shards(): lax.all_to_all(mixed, 'ctx', split_axis=1, concat_axis=0, tiled=True)  15.2 us
    dot_general x1, matrix products, shards(): jnp.einsum('dsc,td->sct', lax.all_gather(in_weight, 'ctx', axis=0, tiled=...  8.06 us
  transfers between devices with their start and end apart: 5, of which 4 were waited for; matrix products, arithmetic and copies ran while one was open for 20% of the time, Pallas kernels for 0%

commit v1 on v0

--- a/solution.py
+++ b/solution.py
@@ -1,10 +1,12 @@
+import functools
 import math
 
 import jax
 import jax.numpy as jnp
 from jax import lax
+from jax.experimental import pallas as pl
+from jax.experimental.pallas import tpu as pltpu
 from jax.sharding import PartitionSpec as P
-
 
 def contract(form, left, right):
     return jnp.einsum(form, left, right, precision=lax.Precision.HIGHEST)
@@ -99,6 +101,398 @@
     )
 
 
+TILE = 128
+MESH = pl.DeviceIdType.MESH
+
+
+def exchange_kernel(
+    planes,
+    packed_ref,
+    tokens_ref,
+    outw_ref,
+    taps_ref,
+    links_ref,
+    out_ref,
+    toks,
+    wide,
+    outw,
+    streams,
+    gated,
+    kernels,
+    bands,
+    mixed,
+    arrived,
+    turned,
+    own_part,
+    sent_part,
+    got_part,
+    local_sem,
+    tok_z_send,
+    tok_z_recv,
+    tok_x_send,
+    tok_x_recv,
+    tok_c_send,
+    tok_c_recv,
+    w_send,
+    w_recv,
+    w_y_send,
+    w_y_recv,
+    o_z_send,
+    o_z_recv,
+    o_y_send,
+    o_y_recv,
+    o_c_send,
+    o_c_recv,
+    m_send,
+    m_recv,
+    p_send,
+    p_recv,
+):
+    g = lax.axis_index("groups")
+    k = lax.axis_index("ctx")
+    x = lax.axis_index("chan")
+    z, core = k // 2, k % 2
+    count = 2 * planes
+    blocks = 2 * count
+    lanes = tokens_ref.shape[0] // 2
+    half_o = outw_ref.shape[0] // 2
+
+    def at(group=g, ctx=k, chan=x):
+        return (group, ctx, chan)
+
+    def remote(src, dst, send, recv, where):
+        return pltpu.make_async_remote_copy(
+            src_ref=src,
+            dst_ref=dst,
+            send_sem=send,
+            recv_sem=recv,
+            device_id=where,
+            device_id_type=MESH,
+        )
+
+    barrier = pltpu.get_barrier_semaphore()
+    for step in range(1, count):
+        pl.semaphore_signal(
+            barrier, inc=1, device_id=at(ctx=(k + step) % count), device_id_type=MESH
+        )
+    pl.semaphore_signal(barrier, inc=1, device_id=at(chan=1 - x), device_id_type=MESH)
+    pl.semaphore_signal(barrier, inc=1, device_id=at(group=1 - g), device_id_type=MESH)
+    pl.semaphore_wait(barrier, count + 1)
+
+    other = 2 * z + 1 - core
+
+    def z_at(step):
+        return 2 * ((z + step) % planes) + core
+
+    def z_from(step):
+        return 2 * ((z + planes - step) % planes) + core
+
+    def tok(owner, half):
+        return toks.at[owner, pl.ds(half * lanes, lanes), :]
+
+    def column(owner, half):
+        return wide.at[:, pl.ds(pl.multiple_of((2 * owner + half) * TILE, TILE), TILE)]
+
+    def outw_at(owner, half):
+        return outw.at[owner, pl.ds(half * half_o, half_o), :]
+
+    waits = []
+
+    locals_ = [
+        pltpu.make_async_copy(tokens_ref, toks.at[k], local_sem.at[0]),
+        pltpu.make_async_copy(packed_ref.at[k, 0], column(k, 0), local_sem.at[1]),
+        pltpu.make_async_copy(packed_ref.at[k, 1], column(k, 1), local_sem.at[2]),
+        pltpu.make_async_copy(outw_ref, outw.at[k], local_sem.at[3]),
+    ]
+    for copy in locals_:
+        copy.start()
+
+    w_copies = []
+    for step in range(1, count):
+        to = (k + step) % count
+        copy = remote(
+            packed_ref.at[to, g], column(k, g), w_send.at[step], w_recv.at[step], at(ctx=to)
+        )
+        copy.start()
+        w_copies.append(copy)
+
+    own_half = tokens_ref.at[pl.ds(x * lanes, lanes), :]
+    tz_copies = []
+    for step in range(1, planes):
+        copy = remote(
+            own_half, tok(k, x), tok_z_send.at[step], tok_z_recv.at[step], at(ctx=z_at(step))
+        )
+        copy.start()
+        tz_copies.append(copy)
+    copy = remote(tokens_ref, toks.at[k], tok_c_send.at[0], tok_c_recv.at[0], at(ctx=other))
+    copy.start()
+    waits.append(copy)
+
+    for step in range(1, count):
+        w_copies[step - 1].wait_recv()
+        came = column((k + count - step) % count, g)
+        copy = remote(came, came, w_y_send.at[step], w_y_recv.at[step], at(group=1 - g))
+        copy.start()
+        waits.append(copy)
+
+    tx_copies = []
+    for step in range(1, planes):
+        tz_copies[step - 1].wait_recv()
+        came = tok(z_from(step), x)
+        copy = remote(came, came, tok_x_send.at[step], tok_x_recv.at[step], at(chan=1 - x))
+        copy.start()
+        tx_copies.append(copy)
+        copy = remote(
+            came, came, tok_c_send.at[2 * step - 1], tok_c_recv.at[2 * step - 1], at(ctx=other)
+        )
+        copy.start()
+        waits.append(copy)
+
+    own_o = outw_ref.at[pl.ds(g * half_o, half_o), :]
+    oz_copies = []
+    for step in range(1, planes):
+        copy = remote(
+            own_o, outw_at(k, g), o_z_send.at[step], o_z_recv.at[step], at(ctx=z_at(step))
+        )
+        copy.start()
+        oz_copies.append(copy)
+    oc_copies = []
+    copy = remote(outw_ref, outw.at[k], o_c_send.at[0], o_c_recv.at[0], at(ctx=other))
+    copy.start()
+    oc_copies.append(copy)
+
+    for step in range(1, planes):
+        tx_copies[step - 1].wait_recv()
+        came = tok(z_from(step), 1 - x)
+        copy = remote(
+            came, came, tok_c_send.at[2 * step], tok_c_recv.at[2 * step], at(ctx=other)
+        )
+        copy.start()
+        waits.append(copy)
+    for copy in locals_:
+        copy.wait()
+    for copy in waits:
+        copy.wait_recv()
+    for copy in w_copies + tz_copies + tx_copies + waits:
+        copy.wait_send()
+
+    rows = wide.shape[0]
+    chans = rows // 4
+
+    def project(index, carry):
+        value = lax.dot_general(
+            wide[: 3 * chans, :],
+            toks[index],
+            (((1,), (1,)), ((), ())),
+            preferred_element_type=jnp.float32,
+        )
+        value = value.astype(jnp.bfloat16).astype(jnp.float32)
+        streams[:, 2 * index, :] = value[:, :TILE]
+        streams[:, 2 * index + 1, :] = value[:, TILE:]
+        return carry
+
+    lax.fori_loop(0, count, project, 0)
+    for m in range(blocks):
+        kernels[:, m, :] = wide[3 * chans :, m * TILE : (m + 1) * TILE].astype(jnp.float32)
+
+    group = 8
+    lane = lax.broadcasted_iota(jnp.int32, (group, blocks, TILE), 2)
+
+    def short(index, carry):
+        first = pl.multiple_of(index * group, group)
+        results = []
+        for s in range(3):
+            value = streams[pl.ds(s * chans + first, group)]
+            total = taps_ref[3 * s, pl.ds(first, group), :][:, None, :] * value
+            for lag in (1, 2):
+                rolled = pltpu.roll(value, lag, 2)
+                moved = jnp.where(lane < lag, pltpu.roll(rolled, 1, 1), rolled)
+                kept = jnp.where(links_ref[lag - 1][None] > 0.5, moved, 0.0)
+                total = total + taps_ref[3 * s + lag, pl.ds(first, group), :][:, None, :] * kept
+            results.append(total)
+        gated[pl.ds(first, group), pl.ds(0, blocks), :] = jnp.zeros_like(results[0])
+        gated[pl.ds(first, group), pl.ds(blocks, blocks), :] = results[0] * results[2]
+        streams[pl.ds(chans + first, group)] = results[1]
+        return carry
+
+    lax.fori_loop(0, chans // group, short, 0)
+
+    oy_copies = []
+    for step in range(1, planes):
+        oz_copies[step - 1].wait_recv()
+        came = outw_at(z_from(step), g)
+        copy = remote(came, came, o_y_send.at[step], o_y_recv.at[step], at(group=1 - g))
+        copy.start()
+        oy_copies.append(copy)
+        copy = remote(
+            came, came, o_c_send.at[2 * step - 1], o_c_recv.at[2 * step - 1], at(ctx=other)
+        )
+        copy.start()
+        oc_copies.append(copy)
+
+    ahead = lax.broadcasted_iota(jnp.int32, (TILE, TILE), 1) >= lax.broadcasted_iota(
+        jnp.int32, (TILE, TILE), 0
+    )
+
+    def filter_pair(index, carry):
+        lefts = []
+        for u in range(2):
+            c = 2 * index + u
+            taps = kernels[c]
+            before = jnp.zeros((TILE, TILE), jnp.float32)
+            for m in range(blocks):
+                row = jnp.broadcast_to(taps[m : m + 1, :], (TILE, TILE))
+                turn = pltpu.roll(row, 0, 1, stride=1, stride_axis=0)
+                bands[m * TILE : (m + 1) * TILE, u * TILE : (u + 1) * TILE] = jnp.where(
+                    ahead, turn, before
+                ).astype(jnp.bfloat16)
+                before = turn
+            lefts.append(
+                jnp.concatenate(
+                    [gated[c, pl.ds(blocks - m, blocks), :] for m in range(blocks)], axis=1
+                ).astype(jnp.bfloat16)
+            )
+        value = jnp.dot(
+            jnp.concatenate(lefts, axis=0), bands[...], preferred_element_type=jnp.float32
+        )
+        for u in range(2):
+            c = 2 * index + u
+            part = value[u * blocks : (u + 1) * blocks, u * TILE : (u + 1) * TILE]
+            streams[chans + c] = streams[chans + c] * part
+        return carry
+
+    lax.fori_loop(0, chans // 2, filter_pair, 0)
+    for m in range(blocks):
+        mixed[m // 2, m % 2] = streams[pl.ds(chans, chans), m, :].astype(jnp.bfloat16)
+
+    m_copies = []
+    for step in range(1, count):
+        to = (k + step) % count
+        copy = remote(
+            mixed.at[to], arrived.at[k], m_send.at[step], m_recv.at[step], at(ctx=to)
+        )
+        copy.start()
+        m_copies.append(copy)
+    own_mixed = pltpu.make_async_copy(mixed.at[k], arrived.at[k], local_sem.at[0])
+    own_mixed.start()
+    for step in range(1, planes):
+        oy_copies[step - 1].wait_recv()
+        came = outw_at(z_from(step), 1 - g)
+        copy = remote(
+            came, came, o_c_send.at[2 * step], o_c_recv.at[2 * step], at(ctx=other)
+        )
+        copy.start()
+        oc_copies.append(copy)
+    own_mixed.wait()
+    for copy in m_copies:
+        copy.wait_recv()
+    for owner in range(count):
+        for h in range(2):
+            turned[h, :, owner * chans : (owner + 1) * chans] = (
+                arrived[owner, h].astype(jnp.float32).T.astype(jnp.bfloat16)
+            )
+    for copy in oc_copies:
+        copy.wait_recv()
+    for copy in m_copies + oz_copies + oy_copies + oc_copies:
+        copy.wait_send()
+
+    wide_e = outw_ref.shape[1]
+    for owner in range(count):
+        sent_part[:, owner * wide_e : (owner + 1) * wide_e] = jnp.dot(
+            turned[1 - x], outw[owner], preferred_element_type=jnp.float32
+        ).astype(jnp.bfloat16)
+    copy = remote(sent_part, got_part, p_send.at[0], p_recv.at[0], at(chan=1 - x))
+    copy.start()
+    for owner in range(count):
+        own_part[:, owner * wide_e : (owner + 1) * wide_e] = jnp.dot(
+            turned[x], outw[owner], preferred_element_type=jnp.float32
+        )
+    copy.wait()
+    out_ref[...] = (own_part[...] + got_part[...].astype(jnp.float32)).astype(jnp.bfloat16)
+
+
+def fused(tokens, in_weight, short_taps, filters, doc_lengths, out_weight):
+    count = lax.axis_size("ctx")
+    depth = in_weight.shape[0]
+    chans = in_weight.shape[2] // count
+    span = filters.shape[1]
+    rows, model = tokens.shape
+    seq_len = span * count
+    blocks = seq_len // TILE
+    weights = in_weight.reshape(2, depth // 2, 3, count, chans).transpose(3, 0, 2, 4, 1)
+    weights = weights.reshape(count, 2, 3 * chans, depth // 2)
+    lags = filters.reshape(count, chans, 2, span // 2).transpose(0, 2, 1, 3)
+    packed = jnp.concatenate((weights, lags), 2)
+    taps = lax.dynamic_slice_in_dim(short_taps, lax.axis_index("ctx") * chans, chans, 2)
+    taps = jnp.broadcast_to(
+        taps.astype(jnp.float32).reshape(9, chans)[:, :, None], (9, chans, TILE)
+    )
+    doc_id = document_ids(doc_lengths, seq_len)
+    links = []
+    for lag in (1, 2):
+        links.append(jnp.concatenate((jnp.zeros((lag,), bool), doc_id[lag:] == doc_id[:-lag])))
+    links = jnp.stack(links).astype(jnp.float32).reshape(2, blocks, TILE)
+
+    planes = count // 2
+    dma = pltpu.SemaphoreType.DMA
+    anywhere = pl.BlockSpec(memory_space=pl.ANY)
+    vmem = pl.BlockSpec(memory_space=pltpu.VMEM)
+    return pl.pallas_call(
+        functools.partial(exchange_kernel, planes),
+        out_shape=jax.ShapeDtypeStruct((rows // 2, model), jnp.bfloat16),
+        in_specs=[anywhere, anywhere, anywhere, vmem, vmem],
+        out_specs=vmem,
+        scratch_shapes=[
+            pltpu.VMEM((count, rows, model), jnp.bfloat16),
+            pltpu.VMEM((4 * chans, model), jnp.bfloat16),
+            pltpu.VMEM((count, out_weight.shape[0], out_weight.shape[1]), jnp.bfloat16),
+            pltpu.VMEM((3 * chans, blocks, TILE), jnp.float32),
+            pltpu.VMEM((chans, 2 * blocks, TILE), jnp.float32),
+            pltpu.VMEM((chans, blocks, TILE), jnp.float32),
+            pltpu.VMEM((seq_len, 2 * TILE), jnp.bfloat16),
+            pltpu.VMEM((count, 2, chans, TILE), jnp.bfloat16),
+            pltpu.VMEM((count, 2, chans, TILE), jnp.bfloat16),
+            pltpu.VMEM((2, TILE, count * chans), jnp.bfloat16),
+            pltpu.VMEM((TILE, model), jnp.float32),
+            pltpu.VMEM((TILE, model), jnp.bfloat16),
+            pltpu.VMEM((TILE, model), jnp.bfloat16),
+            dma((4,)),
+        ]
+        + [dma((planes,))] * 4
+        + [dma((2 * planes - 1,))] * 2
+        + [dma((count,))] * 4
+        + [dma((planes,))] * 4
+        + [dma((2 * planes - 1,))] * 2
+        + [dma((count,))] * 2
+        + [dma((1,))] * 2,
+        compiler_params=pltpu.CompilerParams(
+            collective_id=0, has_side_effects=True, vmem_limit_bytes=56 * 1024 * 1024
+        ),
+    )(packed, tokens, out_weight, taps, links)
+
+
+def fits(tokens, in_weight, filters, out_weight):
+    count = lax.axis_size("ctx")
+    rows, model = tokens.shape
+    return (
+        count % 2 == 0
+        and lax.axis_size("chan") == 2
+        and lax.axis_size("groups") == 2
+        and in_weight.shape[0] == 2 * TILE
+        and in_weight.shape[2] == count * TILE
+        and filters.shape[1] == 2 * TILE
+        and rows == 2 * TILE
+        and out_weight.shape[1] * count == model
+        and count * rows * model * 2 <= 16 * 1024 * 1024
+    )
+
+
+def layer(tokens, in_weight, short_taps, filters, doc_lengths, out_weight):
+    if fits(tokens, in_weight, filters, out_weight):
+        return fused(tokens, in_weight, short_taps, filters, doc_lengths, out_weight)
+    return shards(tokens, in_weight, short_taps, filters, doc_lengths, out_weight)
+
+
 def solution(mesh):
     placed = (
         P(("groups", "ctx"), None),
@@ -109,7 +503,7 @@
         P("chan", "ctx"),
     )
     return jax.shard_map(
-        shards,
+        layer,
         mesh=mesh,
         in_specs=placed,
         out_specs=P(("groups", "ctx", "chan"), None),

time: 368 us -> 194 us (0.53); the launches traced: 361 us -> 191 us
  waiting for transfers between devices: 247 us -> 0 us
  Pallas kernels: 0 us -> 180 us
  matrix products: 68.8 us -> 0 us
  between operations: 13.8 us -> 0.05 us
  local copies, waits for them, and re-layouts: 14.5 us -> 6.68 us
  starting transfers between devices: 7.31 us -> 0 us
  other arithmetic: 10.3 us -> 4.37 us
    pallas_call x0 -> x1, Pallas kernels: none -> 180 us  [fused(): pl.pallas_call(functools.partial(exchange_kernel, planes), out_shape=jax....]
    all_gather x2 -> x0, waiting for transfers between devices: 120 us -> none  [the longest x1 120 us: shards(): lax.all_gather(in_weight, 'ctx', axis=0, tiled=True)]
    all_to_all x2 -> x0, waiting for transfers between devices: 95.1 us -> none  [the longest x1 79.9 us: shards(): lax.all_to_all(packed, 'ctx', split_axis=1, concat_axis=2, tiled=True)]
    dot_general x20 -> x0, matrix products: 68.8 us -> none  [the longest x18 55.9 us: contract(): return jnp.einsum(form, left, right, precision=lax.Precision.HIGHEST)]
    reduce_scatter x1 -> x0, waiting for transfers between devices: 30.8 us -> none  [shards(): lax.psum_scatter(partial_out, 'chan', scatter_dimension=0, tiled=True)]
    all_to_all x2 -> x0, starting transfers between devices: 7.23 us -> none  [the longest x1 3.73 us: shards(): lax.all_to_all(packed, 'ctx', split_axis=1, concat_axis=2, tiled=True)]
    convert_element_type x4 -> x1, other arithmetic: 5.97 us -> 0.62 us  [fused(): links = jnp.stack(links).astype(jnp.float32).reshape(2, blocks, TILE)]
  transfers between devices with their start and end apart: 5 -> 0, of which waited for: 4 -> 0; matrix products, arithmetic and copies ran while one was open for 20% -> 0% of each run, Pallas kernels for 0% -> 0%
where the time goes in v1:
time: 194 us; the launch traced here: 191 us
  Pallas kernels  180 us (93%)
  local copies, waits for them, and re-layouts  6.68 us (3%)
  other arithmetic  4.37 us (2%)
    pallas_call x1, Pallas kernels, fused(): pl.pallas_call(functools.partial(exchange_kernel, planes), out_shape=jax....  180 us

profile of v1, /device:TPU:0, one launch (start us, length us, event | category | flops | bytes accessed | tf_op | source)
XLA Modules:
  0.0 191.5 jit_solution(13412737916892608296)
XLA Ops:
  0.0 0.0 copy-start
  0.0 1.3 reshape.45
  1.3 0.9 copy.18
  2.2 0.0 copy-done
  2.2 0.4 copy.16
  2.6 1.1 copy.11
  3.8 0.0 copy-start.1
  3.8 2.6 %pad_maximum_fusion.packed_ref = bf16[8,2,512,128]{3,2,1,0:T(8,128)(2,1)} fusion(bf16[8,2,128,128]{3,2,1,0:T(8,128)(2,1)} %bitcast.20, bf16[8,2,384,128]{3,2,1,0:T(8,128)(2,1)S(1)} %bitcast.19), kind=kLoop, calls=%fused_computation | loop fusion | flops 4194304 | bytes 4194304 | tf_op jit(solution)/shard_map/concatenate | solution.py:425
  6.3 0.7 dynamic-slice_convert_fusion
  7.0 1.0 broadcast_in_dim.13.taps_ref
  8.1 0.0 copy-done.1
  8.1 0.2 reduce-window.8
  8.3 0.1 convert_reduce_fusion
  8.4 0.1 slice_compare_fusion.1
  8.4 0.1 slice_compare_fusion
  8.5 0.1 add_bitcast_fusion
  8.6 0.6 add_convert_fusion.links_ref
  9.2 180.4 %shard_map.64 = bf16[128,2048]{1,0:T(8,128)(2,1)} custom-call(bf16[8,2,512,128]{3,2,1,0:T(8,128)(2,1)} %pad_maximum_fusion.packed_ref, bf16[256,2048]{1,0:T(8,128)(2,1)} %tokens_ref.1, bf16[1024,256]{1,0:T(8,128)(2,1)} %outw_ref.1, f32[9,128,128]{2,1,0:T(8,128)} %broadcast_in_dim.13.taps_ref, f32[2,16,128]{2,1,0:T(8,128)} %add_convert_fusion.links_ref), custom_call_target="tpu_custom_call" | custom-call | tf_op jit(solution)/shard_map/pallas_call | solution.py:440
  189.6 1.9 copy.20
  (1 shorter events, 0.0 us)
Async XLA Ops:
  0.0 2.2 %copy-start = (bf16[256,3,1024]{2,0,1:T(8,128)(2,1)S(1)}, bf16[256,3,1024]{2,0,1:T(8,128)(2,1)}, u32[]{:S(2)}) copy-start(bf16[256,3,1024]{2,0,1:T(8,128)(2,1)} %param.7) | copy-start | bytes 4718596
  3.8 4.3 %copy-start.1 = (s32[4]{0:T(128)S(1)}, s32[4]{0:T(128)}, u32[]{:S(2)}) copy-start(s32[4]{0:T(128)} %param.10) | copy-start | bytes 52

commit v2 on v1

--- a/solution.py
+++ b/solution.py
@@ -127,6 +127,8 @@
     sent_part,
     got_part,
     local_sem,
+    own_send,
+    own_recv,
     tok_z_send,
     tok_z_recv,
     tok_x_send,
@@ -181,12 +183,6 @@
 
     other = 2 * z + 1 - core
 
-    def z_at(step):
-        return 2 * ((z + step) % planes) + core
-
-    def z_from(step):
-        return 2 * ((z + planes - step) % planes) + core
-
     def tok(owner, half):
         return toks.at[owner, pl.ds(half * lanes, lanes), :]
 
@@ -216,17 +212,54 @@
         copy.start()
         w_copies.append(copy)
 
+    sends = []
+
+    def present(side, step):
+        return z >= step if side == 0 else z + step < planes
+
+    def onward(side):
+        return z + 1 < planes if side == 0 else z >= 1
+
+    def origin(side, step):
+        return 2 * (z - step if side == 0 else z + step) + core
+
+    def beyond(side):
+        return at(ctx=2 * (z + 1 if side == 0 else z - 1) + core)
+
+    def hop(side, step, src, block, send, recv):
+        def copy():
+            return remote(
+                src(side, step), block(side, step), send.at[side, step], recv.at[side, step], beyond(side)
+            )
+
+        ready = onward(side)
+        if step > 1:
+            ready = jnp.logical_and(ready, present(side, step - 1))
+
+        @pl.when(ready)
+        def _():
+            copy().start()
+
+        sends.append((ready, copy))
+
+    def when(condition, action):
+        pl.when(condition)(action)
+
+    def tok_here(side, step, half):
+        return tok(origin(side, step), half)
+
     own_half = tokens_ref.at[pl.ds(x * lanes, lanes), :]
-    tz_copies = []
-    for step in range(1, planes):
-        copy = remote(
-            own_half, tok(k, x), tok_z_send.at[step], tok_z_recv.at[step], at(ctx=z_at(step))
-        )
-        copy.start()
-        tz_copies.append(copy)
-    copy = remote(tokens_ref, toks.at[k], tok_c_send.at[0], tok_c_recv.at[0], at(ctx=other))
-    copy.start()
-    waits.append(copy)
+
+    def tok_src(side, step):
+        return own_half if step == 1 else tok_here(side, step - 1, x)
+
+    def tok_dst(side, step):
+        return tok_here(side, step - 1, x)
+
+    for side in range(2):
+        hop(side, 1, tok_src, tok_dst, tok_z_send, tok_z_recv)
+    core_own = remote(tokens_ref, toks.at[k], own_send.at[0], own_recv.at[0], at(ctx=other))
+    core_own.start()
 
     for step in range(1, count):
         w_copies[step - 1].wait_recv()
@@ -235,46 +268,77 @@
         copy.start()
         waits.append(copy)
 
-    tx_copies = []
+    def tok_z(side, step):
+        came = tok_here(side, step, x)
+        return remote(
+            came, came, tok_z_send.at[side, step], tok_z_recv.at[side, step], at(ctx=other)
+        )
+
+    def tok_x(side, step, half):
+        came = tok_here(side, step, half)
+        return remote(
+            came, came, tok_x_send.at[side, step], tok_x_recv.at[side, step], at(chan=1 - x)
+        )
+
+    def tok_c(side, step, half, which):
+        came = tok_here(side, step, half)
+        return remote(
+            came,
+            came,
+            tok_c_send.at[which, side, step],
+            tok_c_recv.at[which, side, step],
+            at(ctx=other),
+        )
+
     for step in range(1, planes):
-        tz_copies[step - 1].wait_recv()
-        came = tok(z_from(step), x)
-        copy = remote(came, came, tok_x_send.at[step], tok_x_recv.at[step], at(chan=1 - x))
-        copy.start()
-        tx_copies.append(copy)
-        copy = remote(
-            came, came, tok_c_send.at[2 * step - 1], tok_c_recv.at[2 * step - 1], at(ctx=other)
-        )
-        copy.start()
-        waits.append(copy)
+        for side in range(2):
+
+            def arrive(side=side, step=step):
+                tok_z(side, step).wait_recv()
+                tok_x(side, step, x).start()
+                tok_c(side, step, x, 0).start()
+
+            when(present(side, step), arrive)
+            if step + 1 < planes:
+                hop(side, step + 1, tok_src, tok_dst, tok_z_send, tok_z_recv)
 
     own_o = outw_ref.at[pl.ds(g * half_o, half_o), :]
-    oz_copies = []
+
+    def outw_here(side, step, half):
+        return outw_at(origin(side, step), half)
+
+    def outw_src(side, step):
+        return own_o if step == 1 else outw_here(side, step - 1, g)
+
+    def outw_dst(side, step):
+        return outw_here(side, step - 1, g)
+
+    for side in range(2):
+        hop(side, 1, outw_src, outw_dst, o_z_send, o_z_recv)
+    core_own_o = remote(outw_ref, outw.at[k], own_send.at[1], own_recv.at[1], at(ctx=other))
+    core_own_o.start()
+
     for step in range(1, planes):
-        copy = remote(
-            own_o, outw_at(k, g), o_z_send.at[step], o_z_recv.at[step], at(ctx=z_at(step))
-        )
-        copy.start()
-        oz_copies.append(copy)
-    oc_copies = []
-    copy = remote(outw_ref, outw.at[k], o_c_send.at[0], o_c_recv.at[0], at(ctx=other))
-    copy.start()
-    oc_copies.append(copy)
-
-    for step in range(1, planes):
-        tx_copies[step - 1].wait_recv()
-        came = tok(z_from(step), 1 - x)
-        copy = remote(
-            came, came, tok_c_send.at[2 * step], tok_c_recv.at[2 * step], at(ctx=other)
-        )
-        copy.start()
-        waits.append(copy)
+        for side in range(2):
+
+            def arrive_x(side=side, step=step):
+                tok_x(side, step, 1 - x).wait_recv()
+                tok_c(side, step, 1 - x, 1).start()
+
+            when(present(side, step), arrive_x)
     for copy in locals_:
         copy.wait()
     for copy in waits:
         copy.wait_recv()
-    for copy in w_copies + tz_copies + tx_copies + waits:
-        copy.wait_send()
+    core_own.wait_recv()
+    for step in range(1, planes):
+        for side in range(2):
+
+            def arrive_c(side=side, step=step):
+                for which in range(2):
+                    tok_c(side, step, which, which).wait_recv()
+
+            when(present(side, step), arrive_c)
 
     rows = wide.shape[0]
     chans = rows // 4
@@ -292,8 +356,7 @@
         return carry
 
     lax.fori_loop(0, count, project, 0)
-    for m in range(blocks):
-        kernels[:, m, :] = wide[3 * chans :, m * TILE : (m + 1) * TILE].astype(jnp.float32)
+    kernels[...] = wide[3 * chans :, :].astype(jnp.float32)
 
     group = 8
     lane = lax.broadcasted_iota(jnp.int32, (group, blocks, TILE), 2)
@@ -317,36 +380,68 @@
 
     lax.fori_loop(0, chans // group, short, 0)
 
-    oy_copies = []
-    for step in range(1, planes):
-        oz_copies[step - 1].wait_recv()
-        came = outw_at(z_from(step), g)
-        copy = remote(came, came, o_y_send.at[step], o_y_recv.at[step], at(group=1 - g))
-        copy.start()
-        oy_copies.append(copy)
-        copy = remote(
-            came, came, o_c_send.at[2 * step - 1], o_c_recv.at[2 * step - 1], at(ctx=other)
-        )
-        copy.start()
-        oc_copies.append(copy)
-
-    ahead = lax.broadcasted_iota(jnp.int32, (TILE, TILE), 1) >= lax.broadcasted_iota(
-        jnp.int32, (TILE, TILE), 0
+    def outw_z(side, step):
+        came = outw_here(side, step, g)
+        return remote(
+            came, came, o_z_send.at[side, step], o_z_recv.at[side, step], at(ctx=other)
+        )
+
+    def outw_y(side, step, half):
+        came = outw_here(side, step, half)
+        return remote(
+            came, came, o_y_send.at[side, step], o_y_recv.at[side, step], at(group=1 - g)
+        )
+
+    def outw_c(side, step, half, which):
+        came = outw_here(side, step, half)
+        return remote(
+            came, came, o_c_send.at[which, side, step], o_c_recv.at[which, side, step], at(ctx=other)
+        )
+
+    def outw_step(step):
+        for side in range(2):
+
+            def arrive(side=side):
+                outw_z(side, step).wait_recv()
+                outw_y(side, step, g).start()
+                outw_c(side, step, g, 0).start()
+
+            when(present(side, step), arrive)
+            if step + 1 < planes:
+                hop(side, step + 1, outw_src, outw_dst, o_z_send, o_z_recv)
+
+    def outw_last(step):
+        for side in range(2):
+
+            def arrive(side=side):
+                outw_y(side, step, 1 - g).wait_recv()
+                outw_c(side, step, 1 - g, 1).start()
+
+            when(present(side, step), arrive)
+
+    thick = 16
+    place = lax.broadcasted_iota(jnp.int32, (thick, TILE), 1) - lax.broadcasted_iota(
+        jnp.int32, (thick, TILE), 0
     )
 
     def filter_pair(index, carry):
         lefts = []
         for u in range(2):
             c = 2 * index + u
-            taps = kernels[c]
-            before = jnp.zeros((TILE, TILE), jnp.float32)
-            for m in range(blocks):
-                row = jnp.broadcast_to(taps[m : m + 1, :], (TILE, TILE))
-                turn = pltpu.roll(row, 0, 1, stride=1, stride_axis=0)
-                bands[m * TILE : (m + 1) * TILE, u * TILE : (u + 1) * TILE] = jnp.where(
-                    ahead, turn, before
-                ).astype(jnp.bfloat16)
-                before = turn
+            taps = jnp.broadcast_to(kernels[pl.ds(c, 1), :], (thick, blocks * TILE))
+            base = pltpu.roll(taps, 0, 1, stride=1, stride_axis=0).astype(jnp.bfloat16)
+            for q in range(TILE // thick):
+                moved = base if q == 0 else pltpu.roll(base, q * thick, 1)
+                for m in range(blocks):
+                    tile = moved[:, m * TILE : (m + 1) * TILE]
+                    if m == 0:
+                        tile = jnp.where(place >= q * thick, tile.astype(jnp.float32), 0.0).astype(
+                            jnp.bfloat16
+                        )
+                    bands[
+                        m * TILE + q * thick : m * TILE + (q + 1) * thick,
+                        u * TILE : (u + 1) * TILE,
+                    ] = tile
             lefts.append(
                 jnp.concatenate(
                     [gated[c, pl.ds(blocks - m, blocks), :] for m in range(blocks)], axis=1
@@ -361,28 +456,35 @@
             streams[chans + c] = streams[chans + c] * part
         return carry
 
-    lax.fori_loop(0, chans // 2, filter_pair, 0)
-    for m in range(blocks):
-        mixed[m // 2, m % 2] = streams[pl.ds(chans, chans), m, :].astype(jnp.bfloat16)
-
+    parts = 4
+    size = chans // parts
     m_copies = []
-    for step in range(1, count):
-        to = (k + step) % count
-        copy = remote(
-            mixed.at[to], arrived.at[k], m_send.at[step], m_recv.at[step], at(ctx=to)
-        )
-        copy.start()
-        m_copies.append(copy)
+    for part in range(parts):
+        lax.fori_loop(part * size // 2, (part + 1) * size // 2, filter_pair, 0)
+        first = part * size
+        for m in range(blocks):
+            mixed[m // 2, m % 2, first : first + size, :] = streams[
+                chans + first : chans + first + size, m, :
+            ].astype(jnp.bfloat16)
+        for step in range(1, count):
+            to = (k + step) % count
+            copy = remote(
+                mixed.at[to, :, pl.ds(first, size), :],
+                arrived.at[k, :, pl.ds(first, size), :],
+                m_send.at[part, step],
+                m_recv.at[part, step],
+                at(ctx=to),
+            )
+            copy.start()
+            m_copies.append(copy)
+        if part + 1 < planes:
+            outw_step(part + 1)
+    for step in range(parts, planes):
+        outw_step(step)
+    for step in range(1, planes):
+        outw_last(step)
     own_mixed = pltpu.make_async_copy(mixed.at[k], arrived.at[k], local_sem.at[0])
     own_mixed.start()
-    for step in range(1, planes):
-        oy_copies[step - 1].wait_recv()
-        came = outw_at(z_from(step), 1 - g)
-        copy = remote(
-            came, came, o_c_send.at[2 * step], o_c_recv.at[2 * step], at(ctx=other)
-        )
-        copy.start()
-        oc_copies.append(copy)
     own_mixed.wait()
     for copy in m_copies:
         copy.wait_recv()
@@ -391,24 +493,61 @@
             turned[h, :, owner * chans : (owner + 1) * chans] = (
                 arrived[owner, h].astype(jnp.float32).T.astype(jnp.bfloat16)
             )
-    for copy in oc_copies:
-        copy.wait_recv()
-    for copy in m_copies + oz_copies + oy_copies + oc_copies:
-        copy.wait_send()
+    core_own_o.wait_recv()
+    for step in range(1, planes):
+        for side in range(2):
+
+            def arrive_oc(side=side, step=step):
+                for which in range(2):
+                    outw_c(side, step, which, which).wait_recv()
+
+            when(present(side, step), arrive_oc)
 
     wide_e = outw_ref.shape[1]
+    p_copies = []
     for owner in range(count):
-        sent_part[:, owner * wide_e : (owner + 1) * wide_e] = jnp.dot(
+        sent_part[owner] = jnp.dot(
             turned[1 - x], outw[owner], preferred_element_type=jnp.float32
         ).astype(jnp.bfloat16)
-    copy = remote(sent_part, got_part, p_send.at[0], p_recv.at[0], at(chan=1 - x))
-    copy.start()
+        copy = remote(
+            sent_part.at[owner], got_part.at[owner], p_send.at[owner], p_recv.at[owner], at(chan=1 - x)
+        )
+        copy.start()
+        p_copies.append(copy)
     for owner in range(count):
-        own_part[:, owner * wide_e : (owner + 1) * wide_e] = jnp.dot(
+        span = slice(owner * wide_e, (owner + 1) * wide_e)
+        own_part[:, span] = jnp.dot(
             turned[x], outw[owner], preferred_element_type=jnp.float32
         )
-    copy.wait()
-    out_ref[...] = (own_part[...] + got_part[...].astype(jnp.float32)).astype(jnp.bfloat16)
+    for owner in range(count):
+        span = slice(owner * wide_e, (owner + 1) * wide_e)
+        p_copies[owner].wait_recv()
+        out_ref[:, span] = (own_part[:, span] + got_part[owner].astype(jnp.float32)).astype(
+            jnp.bfloat16
+        )
+
+    for copy in w_copies + waits + m_copies + p_copies:
+        copy.wait_send()
+    core_own.wait_send()
+    core_own_o.wait_send()
+    for ready, copy in sends:
+
+        def left(copy=copy):
+            copy().wait_send()
+
+        when(ready, left)
+    for step in range(1, planes):
+        for side in range(2):
+
+            def gone(side=side, step=step):
+                tok_x(side, step, x).wait_send()
+                tok_c(side, step, x, 0).wait_send()
+                tok_c(side, step, 1 - x, 1).wait_send()
+                outw_y(side, step, g).wait_send()
+                outw_c(side, step, g, 0).wait_send()
+                outw_c(side, step, 1 - g, 1).wait_send()
+
+            when(present(side, step), gone)
 
 
 def fused(tokens, in_weight, short_taps, filters, doc_lengths, out_weight):
@@ -448,23 +587,25 @@
             pltpu.VMEM((count, out_weight.shape[0], out_weight.shape[1]), jnp.bfloat16),
             pltpu.VMEM((3 * chans, blocks, TILE), jnp.float32),
             pltpu.VMEM((chans, 2 * blocks, TILE), jnp.float32),
-            pltpu.VMEM((chans, blocks, TILE), jnp.float32),
+            pltpu.VMEM((chans, seq_len), jnp.float32),
             pltpu.VMEM((seq_len, 2 * TILE), jnp.bfloat16),
             pltpu.VMEM((count, 2, chans, TILE), jnp.bfloat16),
             pltpu.VMEM((count, 2, chans, TILE), jnp.bfloat16),
             pltpu.VMEM((2, TILE, count * chans), jnp.bfloat16),
             pltpu.VMEM((TILE, model), jnp.float32),
-            pltpu.VMEM((TILE, model), jnp.bfloat16),
-            pltpu.VMEM((TILE, model), jnp.bfloat16),
+            pltpu.VMEM((count, TILE, out_weight.shape[1]), jnp.bfloat16),
+            pltpu.VMEM((count, TILE, out_weight.shape[1]), jnp.bfloat16),
             dma((4,)),
+            dma((2,)),
+            dma((2,)),
         ]
-        + [dma((planes,))] * 4
-        + [dma((2 * planes - 1,))] * 2
+        + [dma((2, planes))] * 4
+        + [dma((2, 2, planes))] * 2
         + [dma((count,))] * 4
-        + [dma((planes,))] * 4
-        + [dma((2 * planes - 1,))] * 2
-        + [dma((count,))] * 2
-        + [dma((1,))] * 2,
+        + [dma((2, planes))] * 4
+        + [dma((2, 2, planes))] * 2
+        + [dma((4, count))] * 2
+        + [dma((count,))] * 2,
         compiler_params=pltpu.CompilerParams(
             collective_id=0, has_side_effects=True, vmem_limit_bytes=56 * 1024 * 1024
         ),

time: 194 us -> 164 us (0.85); the launches traced: 191 us -> 164 us
  Pallas kernels: 180 us -> 153 us
    pallas_call x1, Pallas kernels: 180 us -> 153 us  [fused(): pl.pallas_call(functools.partial(exchange_kernel, planes), out_shape=jax....]
where the time goes in v2:
time: 164 us
  Pallas kernels  153 us (93%)
  local copies, waits for them, and re-layouts  6.68 us (4%)
  other arithmetic  4.37 us (3%)
    pallas_call x1, Pallas kernels, fused(): pl.pallas_call(functools.partial(exchange_kernel, planes), out_shape=jax....  153 us

profile of v2, /device:TPU:0, one launch (start us, length us, event | category | flops | bytes accessed | tf_op | source)
XLA Modules:
  0.0 164.0 jit_solution(13289101020750177179)
XLA Ops:
  0.0 0.0 copy-start
  0.0 1.3 reshape.45
  1.3 0.9 copy.18
  2.2 0.0 copy-done
  2.2 0.4 copy.16
  2.6 1.1 copy.11
  3.8 0.0 copy-start.1
  3.8 2.6 %pad_maximum_fusion.packed_ref = bf16[8,2,512,128]{3,2,1,0:T(8,128)(2,1)} fusion(bf16[8,2,128,128]{3,2,1,0:T(8,128)(2,1)} %bitcast.20, bf16[8,2,384,128]{3,2,1,0:T(8,128)(2,1)S(1)} %bitcast.19), kind=kLoop, calls=%fused_computation | loop fusion | flops 4194304 | bytes 4194304 | tf_op jit(solution)/shard_map/concatenate | solution.py:564
  6.3 0.7 dynamic-slice_convert_fusion
  7.0 1.0 broadcast_in_dim.13.taps_ref
  8.1 0.0 copy-done.1
  8.1 0.2 reduce-window.8
  8.3 0.1 convert_reduce_fusion
  8.4 0.1 slice_compare_fusion.1
  8.4 0.1 slice_compare_fusion
  8.5 0.1 add_bitcast_fusion
  8.6 0.6 add_convert_fusion.links_ref
  9.2 152.9 %shard_map.64 = bf16[128,2048]{1,0:T(8,128)(2,1)} custom-call(bf16[8,2,512,128]{3,2,1,0:T(8,128)(2,1)} %pad_maximum_fusion.packed_ref, bf16[256,2048]{1,0:T(8,128)(2,1)} %tokens_ref.1, bf16[1024,256]{1,0:T(8,128)(2,1)} %outw_ref.1, f32[9,128,128]{2,1,0:T(8,128)} %broadcast_in_dim.13.taps_ref, f32[2,16,128]{2,1,0:T(8,128)} %add_convert_fusion.links_ref), custom_call_target="tpu_custom_call" | custom-call | tf_op jit(solution)/shard_map/pallas_call | solution.py:579
  162.1 1.9 %copy.20 = bf16[128,2048]{1,0:T(8,128)(2,1)} copy(bf16[128,2048]{1,0:T(8,128)(2,1)} %shard_map.64) | data formatting | bytes 1048576
  (1 shorter events, 0.0 us)
Async XLA Ops:
  0.0 2.2 %copy-start = (bf16[256,3,1024]{2,0,1:T(8,128)(2,1)S(1)}, bf16[256,3,1024]{2,0,1:T(8,128)(2,1)}, u32[]{:S(2)}) copy-start(bf16[256,3,1024]{2,0,1:T(8,128)(2,1)} %param.7) | copy-start | bytes 4718596
  3.8 4.3 %copy-start.1 = (s32[4]{0:T(128)S(1)}, s32[4]{0:T(128)}, u32[]{:S(2)}) copy-start(s32[4]{0:T(128)} %param.10) | copy-start | bytes 52

commit v3 on v2

--- a/solution.py
+++ b/solution.py
@@ -108,6 +108,7 @@
 def exchange_kernel(
     planes,
     packed_ref,
+    filters_ref,
     tokens_ref,
     outw_ref,
     taps_ref,
@@ -120,6 +121,7 @@
     gated,
     kernels,
     bands,
+    early,
     mixed,
     arrived,
     turned,
@@ -139,6 +141,10 @@
     w_recv,
     w_y_send,
     w_y_recv,
+    f_send,
+    f_recv,
+    f_y_send,
+    f_y_recv,
     o_z_send,
     o_z_recv,
     o_y_send,
@@ -186,8 +192,19 @@
     def tok(owner, half):
         return toks.at[owner, pl.ds(half * lanes, lanes), :]
 
+    depth3 = packed_ref.shape[2]
+
+    def tile_of(index):
+        return pl.ds(pl.multiple_of(index * TILE, TILE), TILE)
+
     def column(owner, half):
-        return wide.at[:, pl.ds(pl.multiple_of((2 * owner + half) * TILE, TILE), TILE)]
+        return wide.at[pl.ds(0, depth3), tile_of(2 * owner + half)]
+
+    def lag_column(owner, half):
+        return wide.at[pl.ds(depth3, TILE), tile_of(2 * owner + half)]
+
+    def lags_of(owner, half):
+        return filters_ref.at[tile_of(owner), tile_of(half)]
 
     def outw_at(owner, half):
         return outw.at[owner, pl.ds(half * half_o, half_o), :]
@@ -199,9 +216,69 @@
         pltpu.make_async_copy(packed_ref.at[k, 0], column(k, 0), local_sem.at[1]),
         pltpu.make_async_copy(packed_ref.at[k, 1], column(k, 1), local_sem.at[2]),
         pltpu.make_async_copy(outw_ref, outw.at[k], local_sem.at[3]),
+        pltpu.make_async_copy(lags_of(k, 0), lag_column(k, 0), local_sem.at[4]),
+        pltpu.make_async_copy(lags_of(k, 1), lag_column(k, 1), local_sem.at[5]),
     ]
     for copy in locals_:
         copy.start()
+
+    f_copies = []
+    for step in range(1, count):
+        to = (k + step) % count
+        copy = remote(
+            lags_of(to, g), lag_column(k, g), f_send.at[step], f_recv.at[step], at(ctx=to)
+        )
+        copy.start()
+        f_copies.append(copy)
+
+    sends = []
+
+    def present(side, step):
+        return z >= step if side == 0 else z + step < planes
+
+    def onward(side):
+        return z + 1 < planes if side == 0 else z >= 1
+
+    def origin(side, step):
+        return 2 * (z - step if side == 0 else z + step) + core
+
+    def beyond(side):
+        return at(ctx=2 * (z + 1 if side == 0 else z - 1) + core)
+
+    def hop(side, step, src, block, send, recv):
+        def copy():
+            return remote(
+                src(side, step), block(side, step), send.at[side, step], recv.at[side, step], beyond(side)
+            )
+
+        ready = onward(side)
+        if step > 1:
+            ready = jnp.logical_and(ready, present(side, step - 1))
+
+        @pl.when(ready)
+        def _():
+            copy().start()
+
+        sends.append((ready, copy))
+
+    def when(condition, action):
+        pl.when(condition)(action)
+
+    def tok_here(side, step, half):
+        return tok(origin(side, step), half)
+
+    own_half = tokens_ref.at[pl.ds(x * lanes, lanes), :]
+
+    def tok_src(side, step):
+        return own_half if step == 1 else tok_here(side, step - 1, x)
+
+    def tok_dst(side, step):
+        return tok_here(side, step - 1, x)
+
+    for side in range(2):
+        hop(side, 1, tok_src, tok_dst, tok_z_send, tok_z_recv)
+    core_own = remote(tokens_ref, toks.at[k], own_send.at[0], own_recv.at[0], at(ctx=other))
+    core_own.start()
 
     w_copies = []
     for step in range(1, count):
@@ -211,55 +288,13 @@
         )
         copy.start()
         w_copies.append(copy)
-
-    sends = []
-
-    def present(side, step):
-        return z >= step if side == 0 else z + step < planes
-
-    def onward(side):
-        return z + 1 < planes if side == 0 else z >= 1
-
-    def origin(side, step):
-        return 2 * (z - step if side == 0 else z + step) + core
-
-    def beyond(side):
-        return at(ctx=2 * (z + 1 if side == 0 else z - 1) + core)
-
-    def hop(side, step, src, block, send, recv):
-        def copy():
-            return remote(
-                src(side, step), block(side, step), send.at[side, step], recv.at[side, step], beyond(side)
-            )
-
-        ready = onward(side)
-        if step > 1:
-            ready = jnp.logical_and(ready, present(side, step - 1))
-
-        @pl.when(ready)
-        def _():
-            copy().start()
-
-        sends.append((ready, copy))
-
-    def when(condition, action):
-        pl.when(condition)(action)
-
-    def tok_here(side, step, half):
-        return tok(origin(side, step), half)
-
-    own_half = tokens_ref.at[pl.ds(x * lanes, lanes), :]
-
-    def tok_src(side, step):
-        return own_half if step == 1 else tok_here(side, step - 1, x)
-
-    def tok_dst(side, step):
-        return tok_here(side, step - 1, x)
-
-    for side in range(2):
-        hop(side, 1, tok_src, tok_dst, tok_z_send, tok_z_recv)
-    core_own = remote(tokens_ref, toks.at[k], own_send.at[0], own_recv.at[0], at(ctx=other))
-    core_own.start()
+    fy_copies = []
+    for step in range(1, count):
+        f_copies[step - 1].wait_recv()
+        came = lag_column((k + count - step) % count, g)
+        copy = remote(came, came, f_y_send.at[step], f_y_recv.at[step], at(group=1 - g))
+        copy.start()
+        fy_copies.append(copy)
 
     for step in range(1, count):
         w_copies[step - 1].wait_recv()
@@ -267,6 +302,41 @@
         copy = remote(came, came, w_y_send.at[step], w_y_recv.at[step], at(group=1 - g))
         copy.start()
         waits.append(copy)
+
+    thick = 16
+    place = lax.broadcasted_iota(jnp.int32, (thick, TILE), 1) - lax.broadcasted_iota(
+        jnp.int32, (thick, TILE), 0
+    )
+
+    def build(index, band):
+        for u in range(2):
+            taps = jnp.broadcast_to(
+                kernels[pl.ds(2 * index + u, 1), :], (thick, blocks * TILE)
+            )
+            base = pltpu.roll(taps, 0, 1, stride=1, stride_axis=0).astype(jnp.bfloat16)
+            for q in range(TILE // thick):
+                moved = base if q == 0 else pltpu.roll(base, q * thick, 1)
+                for m in range(blocks):
+                    tile = moved[:, m * TILE : (m + 1) * TILE]
+                    if m == 0:
+                        tile = jnp.where(place >= q * thick, tile.astype(jnp.float32), 0.0).astype(
+                            jnp.bfloat16
+                        )
+                    band[
+                        m * TILE + q * thick : m * TILE + (q + 1) * thick,
+                        u * TILE : (u + 1) * TILE,
+                    ] = tile
+
+    def build_early(index, carry):
+        build(index, early.at[index])
+        return carry
+
+    for copy in fy_copies:
+        copy.wait_recv()
+    for copy in locals_[4:]:
+        copy.wait()
+    kernels[...] = wide[depth3:, :].astype(jnp.float32)
+    ahead = early.shape[0] // (planes - 1)
 
     def tok_z(side, step):
         came = tok_here(side, step, x)
@@ -301,6 +371,8 @@
             when(present(side, step), arrive)
             if step + 1 < planes:
                 hop(side, step + 1, tok_src, tok_dst, tok_z_send, tok_z_recv)
+        last = early.shape[0] if step == planes - 1 else step * ahead
+        lax.fori_loop((step - 1) * ahead, last, build_early, 0)
 
     own_o = outw_ref.at[pl.ds(g * half_o, half_o), :]
 
@@ -326,7 +398,47 @@
                 tok_c(side, step, 1 - x, 1).start()
 
             when(present(side, step), arrive_x)
-    for copy in locals_:
+    def outw_z(side, step):
+        came = outw_here(side, step, g)
+        return remote(
+            came, came, o_z_send.at[side, step], o_z_recv.at[side, step], at(ctx=other)
+        )
+
+    def outw_y(side, step, half):
+        came = outw_here(side, step, half)
+        return remote(
+            came, came, o_y_send.at[side, step], o_y_recv.at[side, step], at(group=1 - g)
+        )
+
+    def outw_c(side, step, half, which):
+        came = outw_here(side, step, half)
+        return remote(
+            came, came, o_c_send.at[which, side, step], o_c_recv.at[which, side, step], at(ctx=other)
+        )
+
+    def outw_step(step):
+        for side in range(2):
+
+            def arrive(side=side):
+                outw_z(side, step).wait_recv()
+                outw_y(side, step, g).start()
+                outw_c(side, step, g, 0).start()
+
+            when(present(side, step), arrive)
+            if step + 1 < planes:
+                hop(side, step + 1, outw_src, outw_dst, o_z_send, o_z_recv)
+
+    def outw_last(step):
+        for side in range(2):
+
+            def arrive(side=side):
+                outw_y(side, step, 1 - g).wait_recv()
+                outw_c(side, step, 1 - g, 1).start()
+
+            when(present(side, step), arrive)
+
+    outw_step(1)
+    for copy in locals_[:4]:
         copy.wait()
     for copy in waits:
         copy.wait_recv()
@@ -356,7 +468,8 @@
         return carry
 
     lax.fori_loop(0, count, project, 0)
-    kernels[...] = wide[3 * chans :, :].astype(jnp.float32)
+    if planes > 2:
+        outw_step(2)
 
     group = 8
     lane = lax.broadcasted_iota(jnp.int32, (group, blocks, TILE), 2)
@@ -379,88 +492,48 @@
         return carry
 
     lax.fori_loop(0, chans // group, short, 0)
-
-    def outw_z(side, step):
-        came = outw_here(side, step, g)
-        return remote(
-            came, came, o_z_send.at[side, step], o_z_recv.at[side, step], at(ctx=other)
-        )
-
-    def outw_y(side, step, half):
-        came = outw_here(side, step, half)
-        return remote(
-            came, came, o_y_send.at[side, step], o_y_recv.at[side, step], at(group=1 - g)
-        )
-
-    def outw_c(side, step, half, which):
-        came = outw_here(side, step, half)
-        return remote(
-            came, came, o_c_send.at[which, side, step], o_c_recv.at[which, side, step], at(ctx=other)
-        )
-
-    def outw_step(step):
-        for side in range(2):
-
-            def arrive(side=side):
-                outw_z(side, step).wait_recv()
-                outw_y(side, step, g).start()
-                outw_c(side, step, g, 0).start()
-
-            when(present(side, step), arrive)
-            if step + 1 < planes:
-                hop(side, step + 1, outw_src, outw_dst, o_z_send, o_z_recv)
-
-    def outw_last(step):
-        for side in range(2):
-
-            def arrive(side=side):
-                outw_y(side, step, 1 - g).wait_recv()
-                outw_c(side, step, 1 - g, 1).start()
-
-            when(present(side, step), arrive)
-
-    thick = 16
-    place = lax.broadcasted_iota(jnp.int32, (thick, TILE), 1) - lax.broadcasted_iota(
-        jnp.int32, (thick, TILE), 0
-    )
-
-    def filter_pair(index, carry):
+    for step in range(3, planes):
+        outw_step(step)
+
+    def filter_pair(index, band):
         lefts = []
         for u in range(2):
-            c = 2 * index + u
-            taps = jnp.broadcast_to(kernels[pl.ds(c, 1), :], (thick, blocks * TILE))
-            base = pltpu.roll(taps, 0, 1, stride=1, stride_axis=0).astype(jnp.bfloat16)
-            for q in range(TILE // thick):
-                moved = base if q == 0 else pltpu.roll(base, q * thick, 1)
-                for m in range(blocks):
-                    tile = moved[:, m * TILE : (m + 1) * TILE]
-                    if m == 0:
-                        tile = jnp.where(place >= q * thick, tile.astype(jnp.float32), 0.0).astype(
-                            jnp.bfloat16
-                        )
-                    bands[
-                        m * TILE + q * thick : m * TILE + (q + 1) * thick,
-                        u * TILE : (u + 1) * TILE,
-                    ] = tile
             lefts.append(
                 jnp.concatenate(
-                    [gated[c, pl.ds(blocks - m, blocks), :] for m in range(blocks)], axis=1
+                    [
+                        gated[2 * index + u, pl.ds(blocks - m, blocks), :]
+                        for m in range(blocks)
+                    ],
+                    axis=1,
                 ).astype(jnp.bfloat16)
             )
         value = jnp.dot(
-            jnp.concatenate(lefts, axis=0), bands[...], preferred_element_type=jnp.float32
+            jnp.concatenate(lefts, axis=0), band[...], preferred_element_type=jnp.float32
         )
         for u in range(2):
             c = 2 * index + u
             part = value[u * blocks : (u + 1) * blocks, u * TILE : (u + 1) * TILE]
             streams[chans + c] = streams[chans + c] * part
+
+    def filter_early(index, carry):
+        for slot in range(2):
+            filter_pair(2 * index + slot, early.at[2 * index + slot])
+        return carry
+
+    def filter_quad(index, carry):
+        for slot in range(2):
+            build(2 * index + slot, bands.at[slot])
+            filter_pair(2 * index + slot, bands.at[slot])
         return carry
 
     parts = 4
     size = chans // parts
     m_copies = []
     for part in range(parts):
-        lax.fori_loop(part * size // 2, (part + 1) * size // 2, filter_pair, 0)
+        begin, end = part * size // 4, (part + 1) * size // 4
+        middle = min(max(begin, early.shape[0] // 2), end)
+        lax.fori_loop(begin, middle, filter_early, 0)
+        lax.fori_loop(middle, end, filter_quad, 0)
         first = part * size
         for m in range(blocks):
             mixed[m // 2, m % 2, first : first + size, :] = streams[
@@ -477,12 +550,9 @@
             )
             copy.start()
             m_copies.append(copy)
-        if part + 1 < planes:
-            outw_step(part + 1)
-    for step in range(parts, planes):
-        outw_step(step)
-    for step in range(1, planes):
-        outw_last(step)
+        if part == 1:
+            for step in range(1, planes):
+                outw_last(step)
     own_mixed = pltpu.make_async_copy(mixed.at[k], arrived.at[k], local_sem.at[0])
     own_mixed.start()
     own_mixed.wait()
@@ -526,7 +596,7 @@
             jnp.bfloat16
         )
 
-    for copy in w_copies + waits + m_copies + p_copies:
+    for copy in w_copies + f_copies + fy_copies + waits + m_copies + p_copies:
         copy.wait_send()
     core_own.wait_send()
     core_own_o.wait_send()
@@ -554,14 +624,11 @@
     count = lax.axis_size("ctx")
     depth = in_weight.shape[0]
     chans = in_weight.shape[2] // count
-    span = filters.shape[1]
     rows, model = tokens.shape
-    seq_len = span * count
+    seq_len = filters.shape[1] * count
     blocks = seq_len // TILE
     weights = in_weight.reshape(2, depth // 2, 3, count, chans).transpose(3, 0, 2, 4, 1)
-    weights = weights.reshape(count, 2, 3 * chans, depth // 2)
-    lags = filters.reshape(count, chans, 2, span // 2).transpose(0, 2, 1, 3)
-    packed = jnp.concatenate((weights, lags), 2)
+    packed = weights.reshape(count, 2, 3 * chans, depth // 2)
     taps = lax.dynamic_slice_in_dim(short_taps, lax.axis_index("ctx") * chans, chans, 2)
     taps = jnp.broadcast_to(
         taps.astype(jnp.float32).reshape(9, chans)[:, :, None], (9, chans, TILE)
@@ -579,7 +646,7 @@
     return pl.pallas_call(
         functools.partial(exchange_kernel, planes),
         out_shape=jax.ShapeDtypeStruct((rows // 2, model), jnp.bfloat16),
-        in_specs=[anywhere, anywhere, anywhere, vmem, vmem],
+        in_specs=[anywhere] * 4 + [vmem, vmem],
         out_specs=vmem,
         scratch_shapes=[
             pltpu.VMEM((count, rows, model), jnp.bfloat16),
@@ -588,28 +655,29 @@
             pltpu.VMEM((3 * chans, blocks, TILE), jnp.float32),
             pltpu.VMEM((chans, 2 * blocks, TILE), jnp.float32),
             pltpu.VMEM((chans, seq_len), jnp.float32),
-            pltpu.VMEM((seq_len, 2 * TILE), jnp.bfloat16),
+            pltpu.VMEM((2, seq_len, 2 * TILE), jnp.bfloat16),
+            pltpu.VMEM((24, seq_len, 2 * TILE), jnp.bfloat16),
             pltpu.VMEM((count, 2, chans, TILE), jnp.bfloat16),
             pltpu.VMEM((count, 2, chans, TILE), jnp.bfloat16),
             pltpu.VMEM((2, TILE, count * chans), jnp.bfloat16),
             pltpu.VMEM((TILE, model), jnp.float32),
             pltpu.VMEM((count, TILE, out_weight.shape[1]), jnp.bfloat16),
             pltpu.VMEM((count, TILE, out_weight.shape[1]), jnp.bfloat16),
-            dma((4,)),
+            dma((6,)),
             dma((2,)),
             dma((2,)),
         ]
         + [dma((2, planes))] * 4
         + [dma((2, 2, planes))] * 2
-        + [dma((count,))] * 4
+        + [dma((count,))] * 8
         + [dma((2, planes))] * 4
         + [dma((2, 2, planes))] * 2
         + [dma((4, count))] * 2
         + [dma((count,))] * 2,
         compiler_params=pltpu.CompilerParams(
-            collective_id=0, has_side_effects=True, vmem_limit_bytes=56 * 1024 * 1024
+            collective_id=0, has_side_effects=True, vmem_limit_bytes=60 * 1024 * 1024
         ),
-    )(packed, tokens, out_weight, taps, links)
+    )(packed, filters, tokens, out_weight, taps, links)
 
 
 def fits(tokens, in_weight, filters, out_weight):

time: 164 us -> 151 us (0.921)
  Pallas kernels: 153 us -> 142 us
  other arithmetic: 4.37 us -> 1.81 us
    pallas_call x1, Pallas kernels: 153 us -> 142 us  [fused(): pl.pallas_call(functools.partial(exchange_kernel, planes), out_shape=jax....]
    concatenate x1 -> x0, other arithmetic: 2.56 us -> none  [fused(): packed = jnp.concatenate((weights, lags), 2)]
    reshape x2 -> x0, local copies, waits for them, and re-layouts: 2.18 us -> none  [fused(): lags = filters.reshape(count, chans, 2, span // 2).transpose(0, 2, 1, 3)]
    unnamed x6 -> x4, local copies, waits for them, and re-layouts: 2.34 us -> 3.73 us
where the time goes in v3:
time: 151 us
  Pallas kernels  142 us (94%)
  local copies, waits for them, and re-layouts  6.6 us (4%)
  other arithmetic  1.81 us (1%)
    pallas_call x1, Pallas kernels, fused(): pl.pallas_call(functools.partial(exchange_kernel, planes), out_shape=jax....  142 us
    unnamed x4, local copies, waits for them, and re-layouts  3.73 us

profile of v3, /device:TPU:0, one launch (start us, length us, event | category | flops | bytes accessed | tf_op | source)
XLA Modules:
  0.0 150.7 jit_solution(28591363766664693)
XLA Ops:
  0.0 1.8 %copy.9 = bf16[96,8,8,128]{3,2,1,0:T(8,128)(2,1)S(1)} copy(bf16[96,8,8,128]{3,1,2,0:T(8,128)(2,1)} %bitcast.17) | data formatting | bytes 3145728
  1.9 0.0 copy-start
  1.9 1.8 %copy.8 = bf16[2,128,3,8,128]{1,4,2,0,3:T(8,128)(2,1)} copy(bf16[2,128,3,8,128]{4,3,1,0,2:T(8,128)(2,1)S(1)} %bitcast.15) | data formatting | bytes 3145728 | tf_op jit(solution)/shard_map/reshape | solution.py:630
  3.7 0.7 dynamic-slice_convert_fusion
  4.4 1.0 broadcast_in_dim.13.taps_ref
  5.4 0.0 copy-done
  5.4 0.2 reduce-window.8
  5.6 0.1 convert_reduce_fusion
  5.7 0.1 slice_compare_fusion.1
  5.8 0.1 slice_compare_fusion
  5.8 0.1 add_bitcast_fusion
  5.9 0.6 add_convert_fusion.links_ref
  6.5 142.3 %shard_map.64 = bf16[128,2048]{1,0:T(8,128)(2,1)} custom-call(bf16[8,2,384,128]{3,2,1,0:T(8,128)(2,1)} %bitcast.16, bf16[1024,256]{1,0:T(8,128)(2,1)} %filters_ref.1, bf16[256,2048]{1,0:T(8,128)(2,1)} %tokens_ref.1, bf16[1024,256]{1,0:T(8,128)(2,1)} %outw_ref.1, f32[9,128,128]{2,1,0:T(8,128)} %broadcast_in_dim.13.taps_ref, ...), custom_call_target="tpu_custom_call" | custom-call | tf_op jit(solution)/shard_map/pallas_call | solution.py:646
  148.8 1.9 %copy.11 = bf16[128,2048]{1,0:T(8,128)(2,1)} copy(bf16[128,2048]{1,0:T(8,128)(2,1)} %shard_map.64) | data formatting | bytes 1048576
  (1 shorter events, 0.0 us)
Async XLA Ops:
  1.9 3.6 %copy-start = (s32[4]{0:T(128)S(1)}, s32[4]{0:T(128)}, u32[]{:S(2)}) copy-start(s32[4]{0:T(128)} %param.10) | copy-start | bytes 52
